TPU v7x, 32 devices: a whole 2x2x4 slice. The times are simulated.
32 devices in a mesh: seq: 8 (over z, x), head: 4 (over y, core).
Axes of the slice: x: 2, y: 2, z: 4, core: 2. Of those that a mesh axis runs over, the one named last changes fastest.
Arguments:
- tokens: bfloat16 [2, 4096, 2560], P(None, 'seq'), may hold values from -6 to 6
- gate_weight: bfloat16 [2560, 5120], P(None, 'head'), may hold values from -0.125 to 0.125
- value_weight: bfloat16 [2560, 5120], P(None, 'head'), may hold values from -0.125 to 0.125
- state_weight: bfloat16 [2560, 256], replicated, may hold values from -0.125 to 0.125
- step_weight: bfloat16 [2560, 80], P(None, 'head'), may hold values from -0.125 to 0.125
- value_kernel: float32 [4, 5120], P(None, 'head'), may hold values from -3 to 3
- value_offset: float32 [5120], P('head'), may hold values from -3 to 3
- state_kernel: float32 [4, 256], replicated, may hold values from -3 to 3
- state_offset: float32 [256], replicated, may hold values from -3 to 3
- step_offset: float32 [80], P('head'), may hold values from -2 to 0.5
- decay_rate: float32 [80], P('head'), may hold values from 0.00024414062 to 0.1
- skip_gain: float32 [80], P('head'), may hold values from 0.5 to 2
- norm_gain: float32 [5120], P('head'), may hold values from 0.5 to 1.5
Outputs:
- normed: bfloat16 [2, 4096, 5120], P(None, 'seq', 'head')
All inputs are finite; a program needn't handle non-finite values.
Results may differ from a plain program's by a relative error of at most 0.0054.
Values may be sent and summed in bfloat16 or wider, within the bound.
No kernel may reach another device: no remote copies, remote signals or barrier semaphores. Data moves between devices by JAX's collectives and lax.ppermute only.
A program may use at most 128 MiB of HBM per device.

v0:
```python
import jax
import jax.numpy as jnp
from jax import lax
from jax.sharding import PartitionSpec as P

GROUP = 256
INNER = 5120


EPS = 1e-05


def shifted(value, axis, steps):
    count = lax.axis_size(axis)
    leading, last = (max(0, -steps), min(count, count - steps))
    return lax.ppermute(value, axis, [(source, source + steps) for source in range(leading, last)])


def conv_rows(previous, incoming, kernel, offset):
    joined = jnp.concatenate([previous, incoming], axis=1).astype(jnp.float32)
    length = incoming.shape[1]
    summed = offset + kernel[0] * lax.slice_in_dim(joined, 0, length, axis=1)
    for tap_index in range(1, kernel.shape[0]):
        summed = summed + kernel[tap_index] * lax.slice_in_dim(
            joined, tap_index, tap_index + length, axis=1
        )
    return jax.nn.silu(summed).astype(jnp.bfloat16)


def local(
    tokens,
    gate_weight,
    value_weight,
    state_weight,
    step_weight,
    value_kernel,
    value_offset,
    state_kernel,
    state_offset,
    step_offset,
    decay_rate,
    skip_gain,
    norm_gain,
):
    batch_count, local_rows, model_width = tokens.shape
    local_inner = gate_weight.shape[1]
    local_heads = step_weight.shape[1]
    head_width = local_inner // local_heads
    state_width = state_weight.shape[1] // 2
    rim_rows = value_kernel.shape[0] - 1
    blocks = local_rows // GROUP
    gate_part = jnp.einsum(
        "btd,dc->btc", tokens, gate_weight, preferred_element_type=jnp.float32
    ).astype(jnp.bfloat16)
    values = jnp.einsum(
        "btd,dc->btc", tokens, value_weight, preferred_element_type=jnp.float32
    ).astype(jnp.bfloat16)
    inout_rows = jnp.einsum(
        "btd,dn->btn", tokens, state_weight, preferred_element_type=jnp.float32
    ).astype(jnp.bfloat16)
    step_sizes = jax.nn.softplus(
        jnp.einsum("btd,dh->bth", tokens, step_weight, preferred_element_type=jnp.float32)
        + step_offset
    )
    edge_rows = jnp.concatenate(
        [values[:, local_rows - rim_rows :], inout_rows[:, local_rows - rim_rows :]], axis=2
    )
    before = shifted(edge_rows, "seq", 1)
    value_conv = conv_rows(before[:, :, :local_inner], values, value_kernel, value_offset)
    inout_conv = conv_rows(before[:, :, local_inner:], inout_rows, state_kernel, state_offset)
    b_all = inout_conv[:, :, :state_width]
    c_all = inout_conv[:, :, state_width:]
    log_decay = -step_sizes * decay_rate
    cumulative = jnp.cumsum(
        log_decay.reshape(batch_count, blocks, GROUP, local_heads), axis=2
    ).reshape(batch_count, local_rows, local_heads)
    causal = (jnp.arange(GROUP)[:, None] >= jnp.arange(GROUP)[None, :])[None, :, :, None]
    within_list = []
    local_list = []
    before_list = []
    c_list = []
    memory = jnp.zeros((batch_count, local_heads, head_width, state_width), jnp.float32)
    factor = jnp.ones((batch_count, local_heads), jnp.float32)
    log_total = jnp.zeros((batch_count, local_heads), jnp.float32)
    for block_index in range(blocks):
        lower = block_index * GROUP
        upper = lower + GROUP
        cum_block = cumulative[:, lower:upper]
        step_block = step_sizes[:, lower:upper]
        b_block = b_all[:, lower:upper]
        c_block = c_all[:, lower:upper]
        value_block = value_conv[:, lower:upper].reshape(
            batch_count, GROUP, local_heads, head_width
        )
        scores = jnp.einsum("btn,bsn->bts", c_block, b_block, preferred_element_type=jnp.float32)
        spread = jnp.where(causal, cum_block[:, :, None, :] - cum_block[:, None, :, :], 0.0)
        mixing = jnp.where(
            causal, scores[:, :, :, None] * jnp.exp(spread) * step_block[:, None, :, :], 0.0
        ).astype(jnp.bfloat16)
        within_list.append(
            jnp.einsum("btsh,bshp->bthp", mixing, value_block, preferred_element_type=jnp.float32)
        )
        closing = jnp.exp(cum_block[:, -1:] - cum_block) * step_block
        weighted = (closing[:, :, :, None] * b_block.astype(jnp.float32)[:, :, None, :]).astype(
            jnp.bfloat16
        )
        produced = jnp.einsum(
            "bshp,bshn->bhpn", value_block, weighted, preferred_element_type=jnp.float32
        )
        local_list.append(memory)
        before_list.append(factor)
        c_list.append(c_block.astype(jnp.float32))
        through = jnp.exp(cum_block[:, -1])
        memory = through[:, :, None, None] * memory + produced
        factor = factor * through
        log_total = log_total + cum_block[:, -1]
    flat_state = memory.reshape(batch_count, local_heads, head_width * state_width)[None]
    shares = lax.all_to_all(flat_state, "seq", split_axis=3, concat_axis=0, tiled=True)
    logs = lax.all_gather(log_total[None], "seq", axis=0, tiled=True)
    inclusive = jnp.cumsum(logs, axis=0)
    exclusive = inclusive - logs
    peers = logs.shape[0]
    earlier_mask = (jnp.arange(peers)[:, None] > jnp.arange(peers)[None, :])[:, :, None, None]
    spread = jnp.where(earlier_mask, exclusive[:, None] - inclusive[None, :], 0.0)
    weights = jnp.where(earlier_mask, jnp.exp(spread), 0.0)
    prefix_shares = jnp.einsum("jibh,ibhs->jbhs", weights, shares, precision=lax.Precision.HIGHEST)
    returned = lax.all_to_all(prefix_shares, "seq", split_axis=0, concat_axis=3, tiled=True)
    state_in = returned[0].reshape(batch_count, local_heads, head_width, state_width)
    gated_list = []
    square_list = []
    for block_index in range(blocks):
        lower = block_index * GROUP
        upper = lower + GROUP
        total_state = (
            local_list[block_index] + before_list[block_index][:, :, None, None] * state_in
        )
        carried = jnp.einsum(
            "bhpn,btn->bthp", total_state, c_list[block_index], precision=lax.Precision.HIGHEST
        )
        inside = jnp.exp(cumulative[:, lower:upper])
        value_block = (
            value_conv[:, lower:upper]
            .reshape(batch_count, GROUP, local_heads, head_width)
            .astype(jnp.float32)
        )
        mixture = (
            within_list[block_index]
            + inside[:, :, :, None] * carried
            + skip_gain[None, None, :, None] * value_block
        )
        gated = mixture.reshape(batch_count, GROUP, local_inner) * jax.nn.silu(
            gate_part[:, lower:upper].astype(jnp.float32)
        )
        gated_list.append(gated)
        square_list.append(jnp.sum(gated * gated, axis=-1))
    squares = lax.psum(jnp.concatenate(square_list, axis=-1), "head")
    inverse = lax.rsqrt(squares / INNER + EPS)
    outputs = []
    for block_index in range(blocks):
        lower = block_index * GROUP
        upper = lower + GROUP
        outputs.append(
            (gated_list[block_index] * inverse[:, lower:upper, None] * norm_gain).astype(
                jnp.bfloat16
            )
        )
    return jnp.concatenate(outputs, axis=1)


def solution(mesh):
    return jax.shard_map(
        local,
        mesh=mesh,
        in_specs=(
            P(None, "seq", None),
            P(None, "head"),
            P(None, "head"),
            P(),
            P(None, "head"),
            P(None, "head"),
            P("head"),
            P(),
            P(),
            P("head"),
            P("head"),
            P("head"),
            P("head"),
        ),
        out_specs=P(None, "seq", "head"),
        check_vma=False,
    )
```

profile of v0, /device:TPU:0, one launch (start us, length us, event | category | flops | bytes accessed | tf_op | source)
XLA Modules:
  0.0 208.8 jit_solution(5006365754057305597)
XLA Ops:
  0.0 10.9 %fusion.22 = bf16[2,512,1280]{2,1,0:T(8,128)(2,1)S(1)} fusion(bf16[2,512,2560]{2,1,0:T(8,128)(2,1)} %param.13, bf16[2560,1280]{1,0:T(8,128)(2,1)} %param.15), kind=kOutput, calls=%fused_computation.31 | convolution fusion | flops 6712197120 | bytes 14417920 | tf_op jit(solution)/shard_map/btd,dc->btc/dot_general | solution.py:55
  11.0 0.0 copy-start.25
  11.0 1.5 fusion.52
  12.6 0.0 copy-start.18
  12.6 5.1 %collective-permute-start = (bf16[2,3,1536]{2,1,0:T(4,128)(2,1)S(1)}, bf16[2,3,1536]{2,1,0:T(4,128)(2,1)S(1)}, u32[]{:S(2)}, u32[]{:S(2)}) collective-permute-start(bf16[2,3,1536]{2,1,0:T(4,128)(2,1)S(1)} %pad_maximum_fusion.1), channel_id=1, source_target_pairs={{0,4},{4,8},{8,12},{12,16},{16,20},{20,24},{24,28},{1,5},{5,9},{9,... | collective-permute-start | bytes 55304 | tf_op jit(solution)/shard_map/ppermute | solution.py:16
  17.7 1.5 negate_multiply_fusion
  19.2 0.1 reshape.131
  19.3 0.1 reshape.118
  19.4 2.3 %reduce-window.6 = f32[2,2,20,2,128]{4,2,3,1,0:T(8,128)S(1)} reduce-window(f32[2,2,20,2,128]{4,2,3,1,0:T(8,128)S(1)} %copy.67, f32[]{:T(128)} %constant.21.clone.1), window={size=1x1x1x1x128 pad=0_0x0_0x0_0x0_0x127_0}, to_apply=%region_0.1 | reduce-window | flops 2600960 | bytes 163844 | tf_op jit(solution)/shard_map/reduce-window
  21.7 0.2 slice_reduce_fusion
  22.0 0.1 broadcast_add_fusion
  22.1 0.1 reduce_window_sum.27
  22.2 0.1 reshape.133
  22.3 0.1 fusion.86
  22.4 0.1 copy.71
  22.5 0.1 copy.72
  22.6 0.5 bitcast_exponential_fusion
  23.2 0.5 bitcast_exponential_fusion.1
  23.7 0.7 exponential_multiply_fusion.1
  24.4 0.1 slice_reduce_fusion.4
  24.5 0.1 maximum_convert_fusion.1
  24.6 0.7 multiply_convert_fusion.11
  25.3 0.7 slice_convert_fusion.1
  26.1 0.4 copy-done.8
  26.5 0.5 maximum_convert_fusion
  27.0 0.2 copy-done.20
  27.2 3.4 %multiply_convert_fusion.2 = bf16[2,512,1280]{2,1,0:T(8,128)(2,1)S(1)} fusion(f32[2,515,1280]{2,1,0:T(8,128)S(1)} %maximum_convert_fusion, f32[1280]{0:T(1024)S(1)} %get-tuple-element.9, f32[1280]{0:T(1024)S(1)} %get-tuple-element.10, f32[1280]{0:T(1024)S(1)} %get-tuple-element.8, f32[1280]{0:T(1024)S(1)} %get-tuple-element.7, f32[1280]{0:T(1024)S(1)} %copy-done.20), kind=kLoop, calls=%fused_computation.28 | loop fusion | flops 17039360 | bytes 23618560 | tf_op jit(solution)/shard_map/convert_element_type | solution.py:27
  30.5 0.2 fusion.85
  30.7 1.4 copy.64
  32.2 0.6 copy.73
  32.8 4.3 %fusion.45 = f32[2,20,64,128]{3,2,1,0:T(8,128)S(1)} fusion(bf16[2,256,20,64]{1,3,2,0:T(8,128)(2,1)} %bitcast.99, f32[2,256,128]{2,1,0:T(8,128)} %get-tuple-element.15, f32[2,256,20]{1,2,0:T(8,128)} %get-tuple-element.17, f32[2,20]{1,0:T(2,128)} %get-tuple-element.34), kind=kOutput, calls=%fused_computation.62 | convolution fusion | flops 170721280 | bytes 2924704 | tf_op jit(solution)/shard_map/bshp,bshn->bhpn/dot_general | solution.py:107
  37.1 1.1 copy-done.5
  38.3 2.0 fusion.44
  40.2 6.0 %copy.95 = f32[2,20,64,128]{1,0,3,2:T(2,128)} copy(f32[2,20,64,128]{3,2,1,0:T(8,128)S(1)} %fusion.44) | data formatting | bytes 2621440 | tf_op jit(solution)/shard_map/broadcast_in_dim;reshape | solution.py:117
  46.2 15.9 %reshape.140 = f32[8,1,40960]{2,1,0:T(1,128)} reshape(f32[8192,1,2,20]{3,2,1,0:T(2,128)} %bitcast.92) | data formatting | bytes 2621440
  62.1 4.9 %all-to-all-start = ((f32[8,1,40960]{2,1,0:T(1,128)}), f32[8,1,40960]{2,1,0:T(1,128)S(1)}, u32[]{:S(2)}, u32[]{:S(2)}) async-start(f32[8,1,40960]{2,1,0:T(1,128)} %reshape.140), calls=%async_computation | async-start | bytes 2621440 | tf_op jit(solution)/shard_map/all_to_all | solution.py:118
  67.0 0.1 copy.79
  67.1 35.6 %all-gather = f32[16,1,20]{2,1,0:T(1,128)S(1)} all-gather(f32[2,1,20]{2,1,0:T(1,128)S(1)} %copy.79), channel_id=2, replica_groups=mesh['seq'=8,'head'=4] {'seq'}, dimensions={0}, use_global_device_ids=true | all-gather | bytes 1440 | tf_op jit(solution)/shard_map/all_gather | solution.py:119
  102.8 0.1 copy.81
  102.9 0.1 copy.80
  103.0 0.5 broadcast.56
  103.5 3.8 %reduce.10 = f32[8,40960]{1,0:T(8,128)S(1)} reduce(f32[8,1,40960]{2,1,0:T(1,128)S(1)} %all-to-all-done, f32[]{:T(128)} %broadcast.56), dimensions={1}, to_apply=%all_to_all.24.reduce_sub_computation | reduce | bytes 2621444 | tf_op jit(solution)/shard_map/all_to_all | solution.py:118
  107.3 16.8 %reshape.141 = f32[8192,1,2,20]{3,2,1,0:T(2,128)} reshape(f32[8,40960]{1,0:T(8,128)S(1)} %reduce.10) | data formatting | bytes 2621440
  124.1 7.1 %copy.78 = f32[1,2,20,8,1024]{4,3,2,1,0:T(8,128)S(1)} copy(f32[1,2,20,8,1024]{2,1,4,3,0:T(2,128)} %bitcast.93) | data formatting | bytes 2621440 | tf_op jit(solution)/shard_map/all_to_all | solution.py:118
  131.2 1.3 convolution_bitcast_fusion
  132.5 2.1 copy.82
  134.6 7.1 %all-to-all-start.1 = ((f32[8,2,20,1024]{3,1,2,0:T(2,128)}), f32[8,2,20,1024]{3,1,2,0:T(2,128)S(1)}, u32[]{:S(2)}, u32[]{:S(2)}) async-start(f32[8,2,20,1024]{3,1,2,0:T(2,128)} %copy.82), calls=%async_computation.1 | async-start | bytes 2621440 | tf_op jit(solution)/shard_map/all_to_all | solution.py:127
  141.8 11.9 %fusion.25 = bf16[2,512,1280]{2,1,0:T(8,128)(2,1)} fusion(bf16[2,512,2560]{2,1,0:T(8,128)(2,1)} %param.13, bf16[2560,1280]{1,0:T(8,128)(2,1)} %param.14), kind=kOutput, calls=%fused_computation.32 | convolution fusion | flops 6712197120 | bytes 14417920 | tf_op jit(solution)/shard_map/btd,dc->btc/dot_general | solution.py:52
  153.7 1.0 fusion.69
  154.7 1.0 fusion.72
  155.7 14.9 %all-to-all-done.1 = f32[8,2,20,1024]{3,1,2,0:T(2,128)S(1)} async-done(((f32[8,2,20,1024]{3,1,2,0:T(2,128)}), f32[8,2,20,1024]{3,1,2,0:T(2,128)S(1)}, u32[]{:S(2)}, u32[]{:S(2)}) %all-to-all-start.1) | async-done | bytes 1310752 | tf_op jit(solution)/shard_map/all_to_all | solution.py:127
  170.6 0.8 copy.83
  171.4 0.2 reshape_squeeze.3
  171.6 2.7 %fusion.65 = f32[2,256,20,64]{1,3,2,0:T(8,128)} fusion(f32[2,20,64,128]{3,2,1,0:T(8,128)S(1)} %reshape_squeeze.3, bf16[2,512,256]{2,1,0:T(8,128)(2,1)S(1)} %multiply_convert_fusion.11), kind=kOutput, calls=%fused_computation.90 | convolution fusion | flops 1006632960 | bytes 4063232 | tf_op jit(solution)/shard_map/bhpn,btn->bthp/dot_general | solution.py:137
  174.4 1.2 fusion.49
  175.6 0.0 copy-done.4
  175.6 0.1 copy-done.11
  175.8 4.6 %fusion.38 = f32[2,256,20,64]{1,3,2,0:T(8,128)} fusion(bf16[2,256,20,64]{1,3,2,0:T(8,128)(2,1)S(1)} %bitcast.96, f32[2,256,20,64]{1,3,2,0:T(8,128)S(1)} %fusion.49, f32[2,256,20]{1,2,0:T(8,128)S(1)} %copy-done.16, f32[2,256,20]{1,2,0:T(8,128)S(1)} %copy-done.17, f32[2,256,256]{2,1,0:T(8,128)S(1)} %copy-done.11, pred[256,256]{1,0:T(8,128)(4,1)S(1)} %iota_compare_fusion, ...), kind=kOutput, calls=%fused_computation.50 | convolution fusion | flops 354549760 | bytes 7266384 | tf_op jit(solution)/shard_map/btsh,bshp->bthp/dot_general | solution.py:101
  180.4 3.3 %copy.85 = f32[2,256,1280]{2,1,0:T(8,128)} copy(f32[2,256,1280]{1,2,0:T(8,128)} %bitcast.98) | data formatting | bytes 5242880 | tf_op jit(solution)/shard_map/reshape | solution.py:151
  183.8 6.1 %fusion.39 = f32[2,256,20,64]{1,3,2,0:T(8,128)} fusion(bf16[2,256,20,64]{1,3,2,0:T(8,128)(2,1)S(1)} %bitcast.100, f32[2,256,20,64]{1,3,2,0:T(8,128)} %fusion.65, f32[2,256,20]{1,2,0:T(8,128)S(1)} %get-tuple-element.21, f32[2,256,20]{1,2,0:T(8,128)S(1)} %copy-done.14, f32[2,256,256]{2,1,0:T(8,128)S(1)} %copy-done.10, ...), kind=kOutput, calls=%fused_computation.52 | convolution fusion | flops 354549760 | bytes 7266384 | tf_op jit(solution)/shard_map/btsh,bshp->bthp/dot_general | solution.py:101
  189.9 3.3 %copy.84 = f32[2,256,1280]{2,1,0:T(8,128)} copy(f32[2,256,1280]{1,2,0:T(8,128)} %bitcast.97) | data formatting | bytes 5242880 | tf_op jit(solution)/shard_map/reshape | solution.py:151
  193.2 4.2 %multiply_reduce_fusion.1 = (f32[2,256]{1,0:T(2,128)S(1)}, f32[2,256]{1,0:T(2,128)S(1)}) fusion(f32[2,256,1280]{2,1,0:T(8,128)} %copy.84, bf16[2,512,1280]{2,1,0:T(8,128)(2,1)} %fusion.25, f32[2,256,1280]{2,1,0:T(8,128)} %copy.85), kind=kLoop, calls=%fused_computation.56 | loop fusion | flops 10484736 | bytes 7868416 | tf_op jit(solution)/shard_map/reduce_sum | solution.py:155
  197.4 5.7 %psum.7 = f32[2,512]{1,0:T(2,128)S(1)} all-reduce(f32[2,512]{1,0:T(2,128)S(1)} %pad_maximum_fusion.2), channel_id=1, replica_groups=mesh['seq'=8,'head'=4] {'head'}, use_global_device_ids=true, to_apply=%region_5.6 | all-reduce | flops 1024 | bytes 8192 | tf_op jit(solution)/shard_map/psum | solution.py:156
  203.1 5.3 %multiply_convert_fusion.6 = (bf16[2,512,1280]{2,1,0:T(8,128)(2,1)}, bf16[2,512,1280]{2,1,0:T(8,128)(2,1)}) fusion(f32[1280]{0:T(1024)S(1)} %copy-done.21, f32[2,256]{1,0:T(2,128)S(1)} %get-tuple-element.27, f32[2,256,1280]{2,1,0:T(8,128)} %copy.84, bf16[2,512,1280]{2,1,0:T(8,128)(2,1)} %fusion.25, ...), kind=kLoop, output_to_operand_aliasing={{0}: (6, {}), {1}: (6, {})}, calls=%fused_computation.54 | loop fusion | flops 11796480 | bytes 10494976 | tf_op jit(solution)/shard_map/convert_element_type | solution.py:163
  (70 shorter events, 0.4 us)
Async XLA Ops:
  0.0 11.0 %copy-start = (bf16[2560,256]{1,0:T(8,128)(2,1)S(1)}, bf16[2560,256]{1,0:T(8,128)(2,1)}, u32[]{:S(2)}) copy-start(bf16[2560,256]{1,0:T(8,128)(2,1)} %param.16) | copy-start | bytes 3932164
  0.0 11.0 %copy-start.2 = (bf16[2,512,2560]{2,1,0:T(8,128)(2,1)S(1)}, bf16[2,512,2560]{2,1,0:T(8,128)(2,1)}, u32[]{:S(2)}) copy-start(bf16[2,512,2560]{2,1,0:T(8,128)(2,1)} %param.13) | copy-start | bytes 15728644
  10.9 1.6 copy-start.7
  11.0 6.7 %copy-start.12 = (bf16[2560,20]{0,1:T(8,128)(2,1)S(1)}, bf16[2560,20]{0,1:T(8,128)(2,1)}, u32[]{:S(2)}) copy-start(bf16[2560,20]{0,1:T(8,128)(2,1)} %param.17) | copy-start | bytes 307204
  11.0 6.7 %copy-start.24 = (f32[20]{0:T(128)S(1)}, f32[20]{0:T(128)}, u32[]{:S(2)}) copy-start(f32[20]{0:T(128)} %param.23) | copy-start | bytes 244
  11.0 6.7 %copy-start.25 = (f32[20]{0:T(128)S(1)}, f32[20]{0:T(128)}, u32[]{:S(2)}) copy-start(f32[20]{0:T(128)} %param.22) | copy-start | bytes 244
  12.6 10.0 %copy-start.23 = (f32[4,256]{1,0:T(4,128)S(1)}, f32[4,256]{1,0:T(4,128)}, u32[]{:S(2)}) copy-start(f32[4,256]{1,0:T(4,128)} %param.20) | copy-start | bytes 12292
  12.6 11.8 %copy-start.18 = (f32[4,1280]{1,0:T(4,128)S(1)}, f32[4,1280]{1,0:T(4,128)}, u32[]{:S(2)}) copy-start(f32[4,1280]{1,0:T(4,128)} %param.18) | copy-start | bytes 61444
  12.6 11.9 %collective-permute-start = (bf16[2,3,1536]{2,1,0:T(4,128)(2,1)S(1)}, bf16[2,3,1536]{2,1,0:T(4,128)(2,1)S(1)}, u32[]{:S(2)}, u32[]{:S(2)}) collective-permute-start(bf16[2,3,1536]{2,1,0:T(4,128)(2,1)S(1)} %pad_maximum_fusion.1), channel_id=1, source_target_pairs={{0,4},{4,8},{8,12},{12,16},{16,20},{20,24},{24,28},{1,5},{5,9},{9,... | collective-permute-start | bytes 55304 | tf_op jit(solution)/shard_map/ppermute | solution.py:16
  19.2 5.4 %copy-start.26 = (f32[256]{0:T(256)S(1)}, f32[256]{0:T(256)}, u32[]{:S(2)}) copy-start(f32[256]{0:T(256)} %param.21) | copy-start | bytes 3076
  24.6 1.8 copy-start.8
  26.5 0.7 copy-start.20
  32.8 7.5 %copy-start.3 = (bf16[2,256,1280]{1,2,0:T(8,128)(2,1)}, bf16[2,256,1280]{1,2,0:T(8,128)(2,1)S(1)}, u32[]{:S(2)}) copy-start(bf16[2,256,1280]{1,2,0:T(8,128)(2,1)S(1)} %copy.73) | copy-start | bytes 3932164
  32.8 5.5 %copy-start.19 = (f32[2,20]{1,0:T(2,128)S(1)}, f32[2,20]{1,0:T(2,128)}, u32[]{:S(2)}) copy-start(f32[2,20]{1,0:T(2,128)} %bitcast_exponential_fusion.1) | copy-start | bytes 484
  37.1 1.1 copy-start.5
  62.1 40.9 %all-to-all-start = ((f32[8,1,40960]{2,1,0:T(1,128)}), f32[8,1,40960]{2,1,0:T(1,128)S(1)}, u32[]{:S(2)}, u32[]{:S(2)}) async-start(f32[8,1,40960]{2,1,0:T(1,128)} %reshape.140), calls=%async_computation | async-start | bytes 2621440 | tf_op jit(solution)/shard_map/all_to_all | solution.py:118
  134.6 36.0 %all-to-all-start.1 = ((f32[8,2,20,1024]{3,1,2,0:T(2,128)}), f32[8,2,20,1024]{3,1,2,0:T(2,128)S(1)}, u32[]{:S(2)}, u32[]{:S(2)}) async-start(f32[8,2,20,1024]{3,1,2,0:T(2,128)} %copy.82), calls=%async_computation.1 | async-start | bytes 2621440 | tf_op jit(solution)/shard_map/all_to_all | solution.py:127
  171.6 2.7 %copy-start.6 = (f32[2,20,64,128]{3,2,1,0:T(8,128)S(1)}, f32[2,20,64,128]{3,2,1,0:T(8,128)}, u32[]{:S(2)}) copy-start(f32[2,20,64,128]{3,2,1,0:T(8,128)} %copy-done.5) | copy-start | bytes 3932164
  171.6 2.7 %copy-start.22 = (f32[2,20]{1,0:T(2,128)S(1)}, f32[2,20]{1,0:T(2,128)}, u32[]{:S(2)}) copy-start(f32[2,20]{1,0:T(2,128)} %get-tuple-element.33) | copy-start | bytes 484
  174.3 1.3 copy-start.4
  174.3 1.4 copy-start.11
  174.3 1.4 copy-start.15
  174.3 1.4 copy-start.16
  174.3 1.4 copy-start.17
  174.3 1.4 copy-start.27
  180.4 3.4 %copy-start.9 = (bf16[2,256,1280]{1,2,0:T(8,128)(2,1)S(1)}, bf16[2,256,1280]{1,2,0:T(8,128)(2,1)}, u32[]{:S(2)}) copy-start(bf16[2,256,1280]{1,2,0:T(8,128)(2,1)} %copy.64) | copy-start | bytes 3932164
  180.4 3.4 %copy-start.10 = (f32[2,256,256]{2,1,0:T(8,128)S(1)}, f32[2,256,256]{2,1,0:T(8,128)}, u32[]{:S(2)}) copy-start(f32[2,256,256]{2,1,0:T(8,128)} %fusion.72) | copy-start | bytes 1572868
  180.4 3.4 %copy-start.13 = (f32[2,256,20]{1,2,0:T(8,128)S(1)}, f32[2,256,20]{1,2,0:T(8,128)}, u32[]{:S(2)}) copy-start(f32[2,256,20]{1,2,0:T(8,128)} %get-tuple-element.23) | copy-start | bytes 122884
  180.4 3.4 %copy-start.14 = (f32[2,256,20]{1,2,0:T(8,128)S(1)}, f32[2,256,20]{1,2,0:T(8,128)}, u32[]{:S(2)}) copy-start(f32[2,256,20]{1,2,0:T(8,128)} %get-tuple-element.24) | copy-start | bytes 122884
  193.2 9.9 %copy-start.21 = (f32[1280]{0:T(1024)S(1)}, f32[1280]{0:T(1024)}, u32[]{:S(2)}) copy-start(f32[1280]{0:T(1024)} %param.25) | copy-start | bytes 15364
  203.1 5.3 %copy-start.1 = (bf16[2560,256]{1,0:T(8,128)(2,1)S(1)}, bf16[2560,256]{1,0:T(8,128)(2,1)}, u32[]{:S(2)}) copy-start(bf16[2560,256]{1,0:T(8,128)(2,1)} %param.16) | copy-start | bytes 3932164
where the time goes:
time: 213 us; the launch traced here: 209 us
  local copies, waits for them, and re-layouts  61.9 us (29%)
  matrix products  50.2 us (24%)
  blocking collectives  41.3 us (19%)
  other arithmetic  22.5 us (11%)
  starting transfers between devices  17.1 us (8%)
  waiting for transfers between devices  14.9 us (7%)
    all_gather x1, blocking collectives, local(): logs = lax.all_gather(log_total[None], 'seq', axis=0, tiled=True)  35.6 us
    unnamed x58, local copies, waits for them, and re-layouts  34.7 us
    all_to_all x1, waiting for transfers between devices, local(): lax.all_to_all(prefix_shares, 'seq', split_axis=0, concat_axis=3, tiled=T...  14.9 us
    dot_general x1, matrix products, local(): jnp.einsum('btd,dc->btc', tokens, gate_weight, preferred_element_type=jnp...  11.9 us
    dot_general x1, matrix products, local(): jnp.einsum('btd,dc->btc', tokens, value_weight, preferred_element_type=jn...  10.9 us
    dot_general x2, matrix products, local(): jnp.einsum('btsh,bshp->bthp', mixing, value_block, preferred_element_type...  10.7 us
    all_to_all x2, local copies, waits for them, and re-layouts, local(): lax.all_to_all(flat_state, 'seq', split_axis=3, concat_axis=0, tiled=True)  7.63 us
    all_to_all x1, starting transfers between devices, local(): lax.all_to_all(prefix_shares, 'seq', split_axis=0, concat_axis=3, tiled=T...  7.15 us
  transfers between devices with their start and end apart: 3, of which 1 were waited for; matrix products, arithmetic and copies ran while one was open for 10% of the time, Pallas kernels for 0%

commit v1 on v0

v1 whole, which is shorter than its diff:
```python
import functools
import jax
import jax.numpy as jnp
from jax import lax
from jax.experimental import pallas as pl
from jax.experimental.pallas import tpu as pltpu
from jax.sharding import PartitionSpec as P

EPS = 1e-05
LOG2E = 1.4426950408889634
PAD = 16
CHUNK = 128
TILE = 256
F32 = jnp.float32
BF16 = jnp.bfloat16


def mm(a, b):
    return jnp.dot(a, b, preferred_element_type=F32)


def halves(x):
    hi = x.astype(BF16)
    return hi, (x - hi.astype(F32)).astype(BF16)


def silu(x):
    return x * (1.0 / (1.0 + jnp.exp(-x)))


def spread(x, select):
    hi, lo = halves(x)
    return mm(hi, select) + mm(lo, select)


def head_select(heads, width, head_width, first_head):
    row = lax.broadcasted_iota(jnp.int32, (heads, width), 0)
    col = lax.broadcasted_iota(jnp.int32, (heads, width), 1)
    start = (row - first_head) * head_width
    return jnp.where((col >= start) & (col < start + head_width), 1.0, 0.0).astype(BF16)


def conv_of(ref, rows, kernel, offset):
    taps = kernel.shape[0]
    total = offset
    for k in range(taps):
        total = total + kernel[k : k + 1, :] * ref[pl.ds(PAD - taps + 1 + k, rows), :]
    return silu(total).astype(BF16)


def front_kernel(tok, sw, tw, toff, rate, io_out, dt_out, cum_out, cumt_out, dtt_out):
    x = tok[0]
    rows = x.shape[0]
    io_out[0] = mm(x, sw[...]).astype(BF16)
    z = mm(x, tw[...]) + toff[...]
    dt = jnp.maximum(z, 0.0) + jnp.log1p(jnp.exp(-jnp.abs(z)))
    dt_out[0] = dt
    log_decay = dt * (rate[...] * (-LOG2E))
    r = lax.broadcasted_iota(jnp.int32, (CHUNK, CHUNK), 0)
    c = lax.broadcasted_iota(jnp.int32, (CHUNK, CHUNK), 1)
    tri = jnp.where(r >= c, 1.0, 0.0).astype(BF16)
    for q in range(rows // CHUNK):
        part = log_decay[q * CHUNK : (q + 1) * CHUNK]
        hi = part.astype(BF16)
        rest = part - hi.astype(F32)
        mid = rest.astype(BF16)
        low = (rest - mid.astype(F32)).astype(BF16)
        cum = mm(tri, hi) + (mm(tri, mid) + mm(tri, low))
        cum_out[0, pl.ds(q * CHUNK, CHUNK), :] = cum
        cumt_out[0, q] = cum.T
        dtt_out[0, q] = dt[q * CHUNK : (q + 1) * CHUNK].T


def front(tokens, state_weight, step_weight, step_offset, decay_rate):
    b, t, d = tokens.shape
    n2, h = state_weight.shape[1], step_weight.shape[1]
    rows = min(t, 256)
    nc = rows // CHUNK
    return pl.pallas_call(
        front_kernel,
        grid=(b, t // rows),
        in_specs=[
            pl.BlockSpec((1, rows, d), lambda i, j: (i, j, 0)),
            pl.BlockSpec((d, n2), lambda i, j: (0, 0)),
            pl.BlockSpec((d, h), lambda i, j: (0, 0)),
            pl.BlockSpec((1, h), lambda i, j: (0, 0)),
            pl.BlockSpec((1, h), lambda i, j: (0, 0)),
        ],
        out_specs=[
            pl.BlockSpec((1, rows, n2), lambda i, j: (i, j, 0)),
            pl.BlockSpec((1, rows, h), lambda i, j: (i, j, 0)),
            pl.BlockSpec((1, rows, h), lambda i, j: (i, j, 0)),
            pl.BlockSpec((1, nc, h, CHUNK), lambda i, j: (i, j, 0, 0)),
            pl.BlockSpec((1, nc, h, CHUNK), lambda i, j: (i, j, 0, 0)),
        ],
        out_shape=[
            jax.ShapeDtypeStruct((b, t, n2), BF16),
            jax.ShapeDtypeStruct((b, t, h), F32),
            jax.ShapeDtypeStruct((b, t, h), F32),
            jax.ShapeDtypeStruct((b, t // CHUNK, h, CHUNK), F32),
            jax.ShapeDtypeStruct((b, t // CHUNK, h, CHUNK), F32),
        ],
        name="front",
        cost_estimate=pl.CostEstimate(
            flops=2 * b * t * d * (n2 + h), transcendentals=0, bytes_accessed=2 * b * t * d
        ),
    )(tokens, state_weight, step_weight, step_offset, decay_rate)


def maps_kernel(io, halo, sw, kern, off, bt_out, b_out, c_out, buf):
    rows = io.shape[1]
    n = sw.shape[1] // 2
    buf[pl.ds(0, PAD), :] = mm(halo[0], sw[...]).astype(BF16).astype(F32)
    buf[pl.ds(PAD, rows), :] = io[0].astype(F32)
    y = conv_of(buf, rows, kern[...], off[...])
    b_out[0] = y[:, :n]
    c_out[0] = y[:, n:]
    bt_out[0] = y[:, :n].astype(F32).T.astype(BF16)


def maps(io, halo, state_weight, kernel, offset):
    b, t, n2 = io.shape
    d = halo.shape[2]
    n = n2 // 2
    return pl.pallas_call(
        maps_kernel,
        grid=(b,),
        in_specs=[
            pl.BlockSpec((1, t, n2), lambda i: (i, 0, 0)),
            pl.BlockSpec((1, PAD, d), lambda i: (i, 0, 0)),
            pl.BlockSpec((d, n2), lambda i: (0, 0)),
            pl.BlockSpec(kernel.shape, lambda i: (0, 0)),
            pl.BlockSpec((1, n2), lambda i: (0, 0)),
        ],
        out_specs=[
            pl.BlockSpec((1, n, t), lambda i: (i, 0, 0)),
            pl.BlockSpec((1, t, n), lambda i: (i, 0, 0)),
            pl.BlockSpec((1, t, n), lambda i: (i, 0, 0)),
        ],
        out_shape=[
            jax.ShapeDtypeStruct((b, n, t), BF16),
            jax.ShapeDtypeStruct((b, t, n), BF16),
            jax.ShapeDtypeStruct((b, t, n), BF16),
        ],
        scratch_shapes=[pltpu.VMEM((t + PAD, n2), F32)],
        name="maps",
    )(io, halo, state_weight, kernel, offset)


def values_kernel(
    share, first, head_width, tok, halo, w, kern, off, bt, dt, cum,
    vc_out, mid_out, end_out, ext, vbuf, sem,
):
    j = pl.program_id(0)
    b, t, h = dt.shape
    width = w.shape[1]
    n = bt.shape[1]
    chunks = t // CHUNK
    copies = []
    for i in range(b):
        copies.append(pltpu.make_async_copy(halo.at[i], ext.at[i, pl.ds(0, PAD)], sem.at[i, 0]))
        copies.append(pltpu.make_async_copy(tok.at[i], ext.at[i, pl.ds(PAD, t)], sem.at[i, 1]))

    @pl.when(j == 0)
    def _():
        for copy in copies:
            copy.start()
        for copy in copies:
            copy.wait()

    per = width // head_width
    select = head_select(h, width, head_width, (first + j) * per)
    for i in range(b):
        vbuf[i] = mm(ext[i], w[...]).astype(BF16).astype(F32)
        vc = conv_of(vbuf.at[i], t, kern[...], off[...])
        vc_out[i] = vc
        state = jnp.zeros((n, width), F32)
        sums = cum[i]
        last = jnp.concatenate(
            [sums[(q + 1) * CHUNK - 1 : (q + 1) * CHUNK] for q in range(chunks)], axis=0
        )
        through = spread(jnp.exp2(last), select)
        for q in range(chunks):
            span = slice(q * CHUNK, (q + 1) * CHUNK)
            closing = jnp.exp2(last[q : q + 1] - sums[span]) * dt[i, span]
            scaled = (vc[span].astype(F32) * spread(closing, select)).astype(BF16)
            made = mm(bt[i, :, span], scaled)
            if q == 0:
                state = made
            else:
                mid_out[i, q - 1] = state.astype(BF16)
                state = state * through[q : q + 1] + made
        at = i * (end_out.shape[1] // b)
        at = pl.multiple_of(at + j * width, 128)
        end_out[:, pl.ds(at, width)] = state.astype(BF16)


def values(tokens, halo, weight, kernel, offset, bt, dt, cum, share, head_width, first, count):
    b, t, d = tokens.shape
    inner, h, n = weight.shape[1], dt.shape[2], bt.shape[1]
    width = TILE
    chunks = t // CHUNK
    cols = count * width
    return pl.pallas_call(
        functools.partial(values_kernel, share, first, head_width),
        grid=(count,),
        in_specs=[
            pl.BlockSpec(memory_space=pl.ANY),
            pl.BlockSpec(memory_space=pl.ANY),
            pl.BlockSpec((d, width), lambda j: (0, j + first)),
            pl.BlockSpec((kernel.shape[0], width), lambda j: (0, j + first)),
            pl.BlockSpec((1, width), lambda j: (0, j + first)),
            pl.BlockSpec((b, n, t), lambda j: (0, 0, 0)),
            pl.BlockSpec((b, t, h), lambda j: (0, 0, 0)),
            pl.BlockSpec((b, t, h), lambda j: (0, 0, 0)),
        ],
        out_specs=[
            pl.BlockSpec((b, t, width), lambda j: (0, 0, j)),
            pl.BlockSpec((b, chunks - 1, n, width), lambda j: (0, 0, 0, j)),
            pl.BlockSpec((n, b * cols), lambda j: (0, 0)),
        ],
        out_shape=[
            jax.ShapeDtypeStruct((b, t, cols), BF16),
            jax.ShapeDtypeStruct((b, chunks - 1, n, cols), BF16),
            jax.ShapeDtypeStruct((n, b * cols), BF16),
        ],
        scratch_shapes=[
            pltpu.VMEM((b, t + PAD, d), BF16),
            pltpu.VMEM((b, t + PAD, width), F32),
            pltpu.SemaphoreType.DMA((b, 2)),
        ],
        name="values",
        cost_estimate=pl.CostEstimate(
            flops=2 * b * t * d * cols, transcendentals=0, bytes_accessed=2 * d * cols
        ),
    )(tokens, halo, weight, kernel, offset, bt, dt, cum)


def gate_kernel(tok, w, out):
    for i in range(tok.shape[0]):
        out[i] = mm(tok[i], w[...]).astype(BF16)


def gate(tokens, weight):
    b, t, d = tokens.shape
    inner = weight.shape[1]
    return pl.pallas_call(
        gate_kernel,
        grid=(inner // TILE,),
        in_specs=[
            pl.BlockSpec((b, t, d), lambda j: (0, 0, 0), pipeline_mode=pl.Buffered(1)),
            pl.BlockSpec((d, TILE), lambda j: (0, j)),
        ],
        out_specs=pl.BlockSpec((b, t, TILE), lambda j: (0, 0, j)),
        out_shape=jax.ShapeDtypeStruct((b, t, inner), BF16),
        name="gate",
        cost_estimate=pl.CostEstimate(
            flops=2 * b * t * d * inner, transcendentals=0, bytes_accessed=2 * d * inner
        ),
    )(tokens, weight)


def inside_kernel(
    head_width, b_rows, c_rows, vc, mid, dtt, cum, cumt, base, skip, gate_rows, part_out, grow_out
):
    q = pl.program_id(1)
    h = cum.shape[2]
    width = vc.shape[2]
    crow = c_rows[0]
    r = lax.broadcasted_iota(jnp.int32, (CHUNK, CHUNK), 0)
    s = lax.broadcasted_iota(jnp.int32, (CHUNK, CHUNK), 1)
    scores = lax.dot_general(
        crow, b_rows[0], (((1,), (1,)), ((), ())), preferred_element_type=F32
    )
    scores = jnp.where(r >= s, scores, 0.0)
    sums = cum[0]
    select = head_select(h, width, head_width, 0)
    rise = spread(jnp.exp2(sums), select)
    lane = lax.broadcasted_iota(jnp.int32, (CHUNK, 2 * head_width), 1)
    carried = mm(crow, mid[0, 0]) * jnp.where(q > 0, 1.0, 0.0)
    silu_gate = silu(gate_rows[0].astype(F32))
    grow_out[0] = (silu_gate * spread(jnp.exp2(sums + base[0, 0]), select)).astype(BF16)
    for pair in range(h // 2):
        at = slice(pair * 2 * head_width, (pair + 1) * 2 * head_width)
        rows = vc[0, :, at]
        mixes = []
        parts = []
        for k in range(2):
            head = 2 * pair + k
            gap = jnp.minimum(sums[:, head : head + 1] - cumt[0, 0, head : head + 1, :], 0.0)
            mixes.append((scores * jnp.exp2(gap) * dtt[0, 0, head : head + 1, :]).astype(BF16))
            parts.append(jnp.where((lane >= head_width) == (k == 1), rows, jnp.zeros_like(rows)))
        within = mm(jnp.concatenate(mixes, axis=1), jnp.concatenate(parts, axis=0))
        mixture = within + rise[:, at] * carried[:, at] + skip[:, at] * rows.astype(F32)
        part_out[0, :, at] = mixture * silu_gate[:, at]


def inside(b_rows, c_rows, vc, mid, dtt, cum, cumt, base, skip, gate_rows, head_width):
    b, t, n = b_rows.shape
    inner, h = vc.shape[2], cum.shape[2]
    return pl.pallas_call(
        functools.partial(inside_kernel, head_width),
        grid=(b, t // CHUNK),
        in_specs=[
            pl.BlockSpec((1, CHUNK, n), lambda i, q: (i, q, 0)),
            pl.BlockSpec((1, CHUNK, n), lambda i, q: (i, q, 0)),
            pl.BlockSpec((1, CHUNK, inner), lambda i, q: (i, q, 0)),
            pl.BlockSpec((1, 1, n, inner), lambda i, q: (i, jnp.maximum(q - 1, 0), 0, 0)),
            pl.BlockSpec((1, 1, h, CHUNK), lambda i, q: (i, q, 0, 0)),
            pl.BlockSpec((1, CHUNK, h), lambda i, q: (i, q, 0)),
            pl.BlockSpec((1, 1, h, CHUNK), lambda i, q: (i, q, 0, 0)),
            pl.BlockSpec((1, 1, 1, h), lambda i, q: (i, q, 0, 0)),
            pl.BlockSpec((1, inner), lambda i, q: (0, 0)),
            pl.BlockSpec((1, CHUNK, inner), lambda i, q: (i, q, 0)),
        ],
        out_specs=[
            pl.BlockSpec((1, CHUNK, inner), lambda i, q: (i, q, 0)),
            pl.BlockSpec((1, CHUNK, inner), lambda i, q: (i, q, 0)),
        ],
        out_shape=[
            jax.ShapeDtypeStruct((b, t, inner), F32),
            jax.ShapeDtypeStruct((b, t, inner), BF16),
        ],
        name="inside",
        cost_estimate=pl.CostEstimate(
            flops=12 * b * t * CHUNK * inner, transcendentals=b * t * CHUNK * h, bytes_accessed=12 * b * t * inner
        ),
    )(b_rows, c_rows, vc, mid, dtt, cum, cumt, base, skip, gate_rows)


def prefix_kernel(came, logs, out):
    peers = came.shape[0]
    through = jnp.exp2(logs[...])
    state = jnp.zeros(came.shape[1:], F32)
    for i in range(peers):
        out[i] = state.astype(BF16)
        if i + 1 < peers:
            state = state * through[i : i + 1] + came[i].astype(F32)


def prefix(came, logs):
    return pl.pallas_call(
        prefix_kernel,
        out_shape=jax.ShapeDtypeStruct(came.shape, BF16),
        name="prefix",
    )(came, logs)


def enter_kernel(part, grow, c_rows, state, out, sq_out):
    total = part[0] + grow[0].astype(F32) * mm(c_rows[0], state[...])
    out[0] = total
    sq = total * total
    acc = sq[:, :128]
    for k in range(1, sq.shape[1] // 128):
        acc = acc + sq[:, k * 128 : (k + 1) * 128]
    sq_out[...] = jnp.sum(acc.T, axis=0, keepdims=True)


def enter(part, grow, c_rows, state, rows=256):
    b, t, inner = part.shape
    n = c_rows.shape[2]
    per = t // rows
    return pl.pallas_call(
        enter_kernel,
        grid=(b, per),
        in_specs=[
            pl.BlockSpec((1, rows, inner), lambda i, q: (i, q, 0)),
            pl.BlockSpec((1, rows, inner), lambda i, q: (i, q, 0)),
            pl.BlockSpec((1, rows, n), lambda i, q: (i, q, 0)),
            pl.BlockSpec((n, inner), lambda i, q: (0, i)),
        ],
        out_specs=[
            pl.BlockSpec((1, rows, inner), lambda i, q: (i, q, 0)),
            pl.BlockSpec((1, rows), lambda i, q: (0, i * per + q)),
        ],
        out_shape=[
            jax.ShapeDtypeStruct((b, t, inner), F32),
            jax.ShapeDtypeStruct((1, b * t), F32),
        ],
        name="enter",
    )(part, grow, c_rows, state)


def norm_kernel(inner_all, count, *refs):
    squares = refs[:count]
    x, gain, out = refs[count:]
    total = squares[0][...]
    for ref in squares[1:]:
        total = total + ref[...]
    inverse = lax.rsqrt(total / inner_all + EPS)
    rows = x.shape[1]
    columns = jnp.broadcast_to(inverse, (128, rows)).T
    for k in range(x.shape[2] // 128):
        at = slice(k * 128, (k + 1) * 128)
        out[0, :, at] = (x[0, :, at] * columns * gain[:, at]).astype(BF16)


def norm(x, squares, gain, inner_all, rows=256):
    b, t, inner = x.shape
    per = t // rows
    return pl.pallas_call(
        functools.partial(norm_kernel, inner_all, len(squares)),
        grid=(b, per),
        in_specs=[pl.BlockSpec((1, rows), lambda i, q: (0, i * per + q)) for _ in squares]
        + [
            pl.BlockSpec((1, rows, inner), lambda i, q: (i, q, 0)),
            pl.BlockSpec((1, inner), lambda i, q: (0, 0)),
        ],
        out_specs=pl.BlockSpec((1, rows, inner), lambda i, q: (i, q, 0)),
        out_shape=jax.ShapeDtypeStruct((b, t, inner), BF16),
        name="norm",
    )(*squares, x, gain)


def local(
    tokens,
    gate_weight,
    value_weight,
    state_weight,
    step_weight,
    value_kernel,
    value_offset,
    state_kernel,
    state_offset,
    step_offset,
    decay_rate,
    skip_gain,
    norm_gain,
):
    b, t, d = tokens.shape
    inner = gate_weight.shape[1]
    h = step_weight.shape[1]
    head_width = inner // h
    peers = lax.axis_size("seq")
    ranks = lax.axis_size("head")
    chunks = t // CHUNK
    halo = lax.ppermute(tokens[:, t - PAD :], "seq", [(i, i + 1) for i in range(peers - 1)])
    io, dt, cum, cumt, dtt = front(
        tokens, state_weight, step_weight, step_offset[None], decay_rate[None]
    )
    last = cum[:, CHUNK - 1 :: CHUNK]
    running = jnp.cumsum(last, axis=1)
    base = (running - last)[:, :, None, :]
    log_total = jnp.repeat(running[:, -1], head_width, axis=1).reshape(1, b * inner)
    logs = lax.all_gather(log_total, "seq", axis=0, tiled=True)
    bt, b_rows, c_rows = maps(io, halo, state_weight, state_kernel, state_offset[None])
    vc, mid, end = values(
        tokens, halo, value_weight, value_kernel, value_offset[None], bt, dt, cum,
        None, head_width, 0, inner // TILE,
    )
    n = end.shape[0]
    came = lax.all_to_all(
        end.reshape(peers, n // peers, b * inner), "seq", split_axis=0, concat_axis=0, tiled=True
    )
    gate_rows = gate(tokens, gate_weight)
    back = lax.all_to_all(prefix(came, logs), "seq", split_axis=0, concat_axis=0, tiled=True)
    skip = jnp.repeat(skip_gain, head_width)[None]
    part, grow = inside(
        b_rows, c_rows, vc, mid, dtt, cum, cumt, base, skip, gate_rows, head_width
    )
    x, sq = enter(part, grow, c_rows, back.reshape(n, b * inner))
    squares = [sq] + [
        lax.ppermute(sq, "head", [(i, (i + k) % ranks) for i in range(ranks)])
        for k in range(1, ranks)
    ]
    return norm(x, squares, norm_gain[None], inner * ranks)


def solution(mesh):
    return jax.shard_map(
        local,
        mesh=mesh,
        in_specs=(
            P(None, "seq", None),
            P(None, "head"),
            P(None, "head"),
            P(),
            P(None, "head"),
            P(None, "head"),
            P("head"),
            P(),
            P(),
            P("head"),
            P("head"),
            P("head"),
            P("head"),
        ),
        out_specs=P(None, "seq", "head"),
        check_vma=False,
    )
```

time: 213 us -> 145 us (0.68); the launches traced: 209 us -> 144 us
  Pallas kernels: 0 us -> 77.3 us
  local copies, waits for them, and re-layouts: 61.9 us -> 10.3 us
  matrix products: 50.2 us -> 0 us
  other arithmetic: 22.5 us -> 0.63 us
  waiting for transfers between devices: 14.9 us -> 0.94 us
  blocking collectives: 41.3 us -> 37.9 us
    pallas_call x0 -> x8, Pallas kernels: none -> 77.3 us  [the longest x1 29.3 us: values(): pl.pallas_call(functools.partial(values_kernel, share, first, head_width)...]
    dot_general x13 -> x0, matrix products: 50.2 us -> none  [the longest x1 11.9 us: local(): jnp.einsum('btd,dc->btc', tokens, gate_weight, preferred_element_type=jnp...]
    unnamed x58 -> x19, local copies, waits for them, and re-layouts: 34.7 us -> 5.66 us
    all_to_all x2, waiting for transfers between devices: 14.9 us -> 0.01 us  [the longest x1 0.01 us: local(): lax.all_to_all(end.reshape(peers, n // peers, b * inner), 'seq', split_ax...]
    convert_element_type x7 -> x0, other arithmetic: 10.7 us -> none  [the longest x2 5.32 us: local(): (gated_list[block_index] * inverse[:, lower:upper, None] * norm_gain).ast...]
    all_to_all x3 -> x0, local copies, waits for them, and re-layouts: 8.39 us -> none  [the longest x2 7.63 us: local(): lax.all_to_all(flat_state, 'seq', split_axis=3, concat_axis=0, tiled=True)]
    reshape x6 -> x0, local copies, waits for them, and re-layouts: 6.85 us -> none  [the longest x2 6.62 us: local(): mixture.reshape(batch_count, GROUP, local_inner)]
    another operation x6 -> x1, local copies, waits for them, and re-layouts: 6.42 us -> 0.67 us  [local(): skip = jnp.repeat(skip_gain, head_width)[None]]
  transfers between devices with their start and end apart: 3 -> 6, of which waited for: 1 -> 2; matrix products, arithmetic and copies ran while one was open for 10% -> 5% of each run, Pallas kernels for 0% -> 21%
where the time goes in v1:
time: 145 us; the launch traced here: 144 us
  Pallas kernels  77.3 us (53%)
  blocking collectives  37.9 us (26%)
  starting transfers between devices  16.3 us (11%)
  local copies, waits for them, and re-layouts  10.3 us (7%)
    all_gather x1, blocking collectives, local(): logs = lax.all_gather(log_total, 'seq', axis=0, tiled=True)  37.9 us
    pallas_call x1, Pallas kernels, values(): pl.pallas_call(functools.partial(values_kernel, share, first, head_width)...  29.3 us
    pallas_call x1, Pallas kernels, inside(): pl.pallas_call(functools.partial(inside_kernel, head_width), grid=(b, t /...  11.6 us
    pallas_call x1, Pallas kernels, gate(): pl.pallas_call(gate_kernel, grid=(inner // TILE,), in_specs=[pl.BlockSpec...  11.4 us
    pallas_call x1, Pallas kernels, front(): pl.pallas_call(front_kernel, grid=(b, t // rows), in_specs=[pl.BlockSpec(...  7.28 us
    pallas_call x1, Pallas kernels, enter(): pl.pallas_call(enter_kernel, grid=(b, per), in_specs=[pl.BlockSpec((1, ro...  6.61 us
    unnamed x19, local copies, waits for them, and re-layouts  5.66 us
    pallas_call x1, Pallas kernels, norm(): pl.pallas_call(functools.partial(norm_kernel, inner_all, len(squares)), g...  4.94 us
  transfers between devices with their start and end apart: 6, of which 2 were waited for; matrix products, arithmetic and copies ran while one was open for 5% of the time, Pallas kernels for 21%

profile of v1, /device:TPU:0, one launch (start us, length us, event | category | flops | bytes accessed | tf_op | source)
XLA Modules:
  0.0 143.5 jit_solution(5194791953888847416)
XLA Ops:
  0.0 0.9 slice.9
  0.9 4.9 %collective-permute-start = (bf16[2,16,2560]{2,1,0:T(8,128)(2,1)S(1)}, bf16[2,16,2560]{2,1,0:T(8,128)(2,1)S(1)}, u32[]{:S(2)}, u32[]{:S(2)}) collective-permute-start(bf16[2,16,2560]{2,1,0:T(8,128)(2,1)S(1)} %slice.9), channel_id=1, source_target_pairs={{0,4},{4,8},{8,12},{12,16},{16,20},{20,24},{24,28},{1,5},{5,9},{9,... | collective-permute-start | bytes 491528 | tf_op jit(solution)/shard_map/ppermute | solution.py:437
  5.8 2.0 %copy.17.tw = bf16[2560,20]{1,0:T(8,128)(2,1)} copy(bf16[2560,20]{0,1:T(8,128)(2,1)} %param.17) | data formatting | bytes 204800 | tf_op args[4]
  7.8 1.3 broadcast_in_dim.27.off
  9.1 7.3 %front.1 = (bf16[2,512,256]{2,1,0:T(8,128)(2,1)}, f32[2,512,20]{2,1,0:T(8,128)}, f32[2,512,20]{2,1,0:T(8,128)}, f32[2,4,20,128]{3,2,1,0:T(8,128)}, f32[2,4,20,128]{3,2,1,0:T(8,128)}) custom-call(bf16[2,512,2560]{2,1,0:T(8,128)(2,1)} %tok.5, bf16[2560,256]{1,0:T(8,128)(2,1)} %sw.3, bf16[2560,20]{1,0:T(8,128)(2,1)} %copy.17.tw, f32[1,20]{1,0:T(1,128)} %bitcast.16, ...), custom_call_target="tpu_custom_call" | custom-call | flops 1447034880 | bytes 5242880 | tf_op jit(solution)/shard_map/front/pallas_call | solution.py:79
  16.4 0.0 collective-permute-done.halo
  16.4 0.0 copy-start.2
  16.4 0.7 copy-done.2
  17.1 4.0 %maps.1 = (bf16[2,128,512]{2,1,0:T(8,128)(2,1)}, bf16[2,512,128]{2,1,0:T(8,128)(2,1)}, bf16[2,512,128]{2,1,0:T(8,128)(2,1)}) custom-call(bf16[2,512,256]{2,1,0:T(8,128)(2,1)} %get-tuple-element.20.io, bf16[2,16,2560]{2,1,0:T(8,128)(2,1)} %copy-done.2, bf16[2560,256]{1,0:T(8,128)(2,1)} %sw.3, f32[4,256]{1,0:T(4,128)} %kern.2, f32[1,256]{1,0:T(1,128)} %bitcast.15), custom_call_target="tpu_custom_call" | custom-call | tf_op jit(solution)/shard_map/maps/pallas_call | solution.py:125
  21.1 29.3 %values.1 = (bf16[2,512,1280]{2,1,0:T(8,128)(2,1)}, bf16[2,3,128,1280]{3,2,1,0:T(8,128)(2,1)}, bf16[128,2560]{1,0:T(8,128)(2,1)}) custom-call(bf16[2,512,2560]{2,1,0:T(8,128)(2,1)} %tok.5, bf16[2,16,2560]{2,1,0:T(8,128)(2,1)} %copy-done.2, bf16[2560,1280]{1,0:T(8,128)(2,1)} %w.2, f32[4,1280]{1,0:T(4,128)} %kern.3, f32[1,1280]{1,0:T(1,128)} %broadcast_in_dim.27.off, ...), custom_call_target="tpu_custom_call" | custom-call | flops 6710886400 | bytes 6553600 | tf_op jit(solution)/shard_map/values/pallas_call | solution.py:204
  50.4 0.0 copy-start.7
  50.4 4.9 %all-to-all-start = ((bf16[8,16,2560]{2,1,0:T(8,128)(2,1)}), bf16[8,16,2560]{2,1,0:T(8,128)(2,1)S(1)}, u32[]{:S(2)}, u32[]{:S(2)}) async-start(bf16[8,16,2560]{2,1,0:T(8,128)(2,1)} %bitcast.11), calls=%async_computation | async-start | bytes 1310720 | tf_op jit(solution)/shard_map/all_to_all | solution.py:452
  55.3 1.0 slice.10
  56.4 0.1 broadcast_in_dim.30
  56.5 0.1 reshape.8
  56.6 37.9 %all-gather = f32[8,1,2560]{2,1,0:T(1,128)S(1)} all-gather(f32[1,1,2560]{2,1,0:T(1,128)S(1)} %reshape.8), channel_id=1, replica_groups=mesh['seq'=8,'head'=4] {'seq'}, dimensions={0}, use_global_device_ids=true | all-gather | bytes 92160 | tf_op jit(solution)/shard_map/all_gather | solution.py:445
  94.5 0.6 copy.20
  95.1 0.0 all-to-all-done.came
  95.1 0.0 copy-start.1
  95.1 0.8 copy-done.1
  96.0 2.1 %prefix.1 = bf16[8,16,2560]{2,1,0:T(8,128)(2,1)} custom-call(bf16[8,16,2560]{2,1,0:T(8,128)(2,1)} %copy-done.1, f32[8,2560]{1,0:T(8,128)} %bitcast.12), custom_call_target="tpu_custom_call" | custom-call | tf_op jit(solution)/shard_map/prefix/pallas_call | solution.py:342
  98.1 3.5 %all-to-all-start.1 = ((bf16[8,16,2560]{2,1,0:T(8,128)(2,1)}), bf16[8,16,2560]{2,1,0:T(8,128)(2,1)S(1)}, u32[]{:S(2)}, u32[]{:S(2)}) async-start(bf16[8,16,2560]{2,1,0:T(8,128)(2,1)} %prefix.1), calls=%async_computation.1 | async-start | bytes 1310720 | tf_op jit(solution)/shard_map/all_to_all | solution.py:456
  101.6 0.6 sub.3
  102.2 0.0 copy-done.7
  102.2 0.1 broadcast_in_dim.29
  102.3 0.7 broadcast_in_dim_reshape.3.skip
  103.0 11.4 %gate.1.gate_rows = bf16[2,512,1280]{2,1,0:T(8,128)(2,1)} custom-call(bf16[2,512,2560]{2,1,0:T(8,128)(2,1)} %tok.5, bf16[2560,1280]{1,0:T(8,128)(2,1)} %w.3), custom_call_target="tpu_custom_call" | custom-call | flops 6710886400 | bytes 6553600 | tf_op jit(solution)/shard_map/gate/pallas_call | solution.py:247
  114.4 11.6 %inside.1 = (f32[2,512,1280]{2,1,0:T(8,128)}, bf16[2,512,1280]{2,1,0:T(8,128)(2,1)}) custom-call(bf16[2,512,128]{2,1,0:T(8,128)(2,1)} %get-tuple-element.21.b_rows, bf16[2,512,128]{2,1,0:T(8,128)(2,1)} %get-tuple-element.22.c_rows, bf16[2,512,1280]{2,1,0:T(8,128)(2,1)} %get-tuple-element.26.vc, bf16[2,3,128,1280]{3,2,1,0:T(8,128)(2,1)} %get-tuple-element.27.mid, ...), custom_call_target="tpu_custom_call" | custom-call | flops 2013265920 | bytes 15728640 | tf_op jit(solution)/shard_map/inside/pallas_call | solution.py:301
  126.0 0.0 all-to-all-done.1
  126.0 0.0 copy-start
  126.0 0.8 copy-done
  126.8 0.0 copy-start.3
  126.8 6.6 %enter.1 = (f32[2,512,1280]{2,1,0:T(8,128)}, f32[1,1024]{1,0:T(1,128)}) custom-call(f32[2,512,1280]{2,1,0:T(8,128)} %get-tuple-element.30.part, bf16[2,512,1280]{2,1,0:T(8,128)(2,1)} %get-tuple-element.31.grow, bf16[2,512,128]{2,1,0:T(8,128)(2,1)} %get-tuple-element.22.c_rows, bf16[128,2560]{1,0:T(8,128)(2,1)} %bitcast.10), custom_call_target="tpu_custom_call" | custom-call | tf_op jit(solution)/shard_map/enter/pallas_call | solution.py:363
  133.5 0.0 collective-permute-start.1
  133.5 1.6 %collective-permute-start.2 = (f32[1,1024]{1,0:T(1,128)}, f32[1,1024]{1,0:T(1,128)S(1)}, u32[]{:S(2)}, u32[]{:S(2)}) collective-permute-start(f32[1,1024]{1,0:T(1,128)} %get-tuple-element.33.refs_0_), channel_id=1, source_target_pairs={{0,2},{1,3},{2,0},{3,1},{4,6},{5,7},{6,4},{7,5},{8,10},{9,11},{10,... | collective-permute-start | bytes 12296 | tf_op jit(solution)/shard_map/ppermute | solution.py:463
  135.1 1.4 collective-permute-start.3
  136.4 0.0 copy-done.3
  136.5 0.6 broadcast_in_dim.31.refs_5_
  137.0 0.0 collective-permute-done.1.refs_1_
  137.0 0.0 copy-start.4
  137.1 0.3 collective-permute-done.2.refs_2_
  137.4 0.0 copy-start.5
  137.4 0.6 collective-permute-done.3.refs_3_
  138.0 0.0 copy-start.6
  138.0 0.0 copy-done.4
  138.0 0.0 copy-done.5
  138.0 0.6 copy-done.6
  138.6 4.9 %norm.1 = bf16[2,512,1280]{2,1,0:T(8,128)(2,1)} custom-call(f32[1,1024]{1,0:T(1,128)} %get-tuple-element.33.refs_0_, f32[1,1024]{1,0:T(1,128)} %copy-done.4, f32[1,1024]{1,0:T(1,128)} %copy-done.5, f32[1,1024]{1,0:T(1,128)} %copy-done.6, f32[2,512,1280]{2,1,0:T(8,128)} %get-tuple-element.34.refs_4_, f32[1,1280]{1,0:T(1,128)} %broadcast_in_dim.31.refs_5_), custom_call_target="tpu_custom_call" | custom-call | tf_op jit(solution)/shard_map/norm/pallas_call | solution.py:401
  (2 shorter events, 0.0 us)
Async XLA Ops:
  0.9 15.5 %collective-permute-start = (bf16[2,16,2560]{2,1,0:T(8,128)(2,1)S(1)}, bf16[2,16,2560]{2,1,0:T(8,128)(2,1)S(1)}, u32[]{:S(2)}, u32[]{:S(2)}) collective-permute-start(bf16[2,16,2560]{2,1,0:T(8,128)(2,1)S(1)} %slice.9), channel_id=1, source_target_pairs={{0,4},{4,8},{8,12},{12,16},{16,20},{20,24},{24,28},{1,5},{5,9},{9,... | collective-permute-start | bytes 491528 | tf_op jit(solution)/shard_map/ppermute | solution.py:437
  16.4 0.7 copy-start.2
  50.4 51.8 %copy-start.7 = (f32[20]{0:T(128)S(1)}, f32[20]{0:T(128)}, u32[]{:S(2)}) copy-start(f32[20]{0:T(128)} %param.24) | copy-start | bytes 244
  50.4 44.7 %all-to-all-start = ((bf16[8,16,2560]{2,1,0:T(8,128)(2,1)}), bf16[8,16,2560]{2,1,0:T(8,128)(2,1)S(1)}, u32[]{:S(2)}, u32[]{:S(2)}) async-start(bf16[8,16,2560]{2,1,0:T(8,128)(2,1)} %bitcast.11), calls=%async_computation | async-start | bytes 1310720 | tf_op jit(solution)/shard_map/all_to_all | solution.py:452
  95.1 0.8 copy-start.1
  98.1 27.9 %all-to-all-start.1 = ((bf16[8,16,2560]{2,1,0:T(8,128)(2,1)}), bf16[8,16,2560]{2,1,0:T(8,128)(2,1)S(1)}, u32[]{:S(2)}, u32[]{:S(2)}) async-start(bf16[8,16,2560]{2,1,0:T(8,128)(2,1)} %prefix.1), calls=%async_computation.1 | async-start | bytes 1310720 | tf_op jit(solution)/shard_map/all_to_all | solution.py:456
  126.0 0.8 copy-start
  126.8 9.6 %copy-start.3 = (f32[1280]{0:T(1024)S(1)}, f32[1280]{0:T(1024)}, u32[]{:S(2)}) copy-start(f32[1280]{0:T(1024)} %param.25) | copy-start | bytes 15364
  133.5 3.6 %collective-permute-start.1 = (f32[1,1024]{1,0:T(1,128)}, f32[1,1024]{1,0:T(1,128)S(1)}, u32[]{:S(2)}, u32[]{:S(2)}) collective-permute-start(f32[1,1024]{1,0:T(1,128)} %get-tuple-element.33.refs_0_), channel_id=1, source_target_pairs={{0,1},{1,2},{2,3},{3,0},{4,5},{5,6},{6,7},{7,4},{8,9},{9,10},{10,1... | collective-permute-start | bytes 12296 | tf_op jit(solution)/shard_map/ppermute | solution.py:463
  133.5 3.9 %collective-permute-start.2 = (f32[1,1024]{1,0:T(1,128)}, f32[1,1024]{1,0:T(1,128)S(1)}, u32[]{:S(2)}, u32[]{:S(2)}) collective-permute-start(f32[1,1024]{1,0:T(1,128)} %get-tuple-element.33.refs_0_), channel_id=1, source_target_pairs={{0,2},{1,3},{2,0},{3,1},{4,6},{5,7},{6,4},{7,5},{8,10},{9,11},{10,... | collective-permute-start | bytes 12296 | tf_op jit(solution)/shard_map/ppermute | solution.py:463
  135.1 2.9 %collective-permute-start.3 = (f32[1,1024]{1,0:T(1,128)}, f32[1,1024]{1,0:T(1,128)S(1)}, u32[]{:S(2)}, u32[]{:S(2)}) collective-permute-start(f32[1,1024]{1,0:T(1,128)} %get-tuple-element.33.refs_0_), channel_id=1, source_target_pairs={{0,3},{1,0},{2,1},{3,2},{4,7},{5,4},{6,5},{7,6},{8,11},{9,8},{10,9... | collective-permute-start | bytes 12296 | tf_op jit(solution)/shard_map/ppermute | solution.py:463
  137.0 0.9 copy-start.4
  137.4 0.6 copy-start.5
  138.0 0.6 copy-start.6
